TPU v7x, 32 devices: a whole 2x2x4 slice. The times are simulated.
32 devices in a mesh: lat: 4 (over z), lon: 8 (over y, x, core).
Axes of the slice: x: 2, y: 2, z: 4, core: 2. Of those that a mesh axis runs over, the one named last changes fastest.
Arguments:
- spectral: bfloat16 [640, 2, 128, 640], P('lat', None, 'lon'), may hold values from -6 to 6
- wavenumber_of_slot: int32 [640], replicated, may hold values from 0 to 639, each once
- filter_strength: float32 [128], P('lon'), may hold values from 0.1 to 10
- courant: bfloat16 [2, 640, 1280, 128], P(None, 'lat', 'lon'), may hold values from -0.59765625 to 0.59765625
- sunlit_blocks: int32 [4, 8, 12], P('lat', 'lon'), may hold values from 0 to 1599, as said below
- sunlit_owner: int32 [4, 8, 12, 1], P('lat', 'lon'), may hold values from 0 to 7; in each aligned block of 12 rows (0 to 11, 12 to 23, ..., all dimensions but the last counted through in order) at most 2 rows name the same one
- radiation_in: bfloat16 [8, 128, 512], P('lon'), may hold values from -0.5 to 0.5
- radiation_mid: bfloat16 [8, 512, 512], P('lon'), may hold values from -0.25 to 0.25
- radiation_out: bfloat16 [8, 512, 128], P('lon'), may hold values from -0.25 to 0.25
Outputs:
- advected: float32 [640, 1280, 128], P('lat', 'lon')
- heating: bfloat16 [640, 1280, 128], P('lat', 'lon')
Inputs may be any that keep to these rules, and one draw needn't show every extreme that they name: `wavenumber_of_slot`: each of 0 to 639 exactly once. `sunlit_blocks`: the 12 block numbers of one device are distinct. `sunlit_owner`: among the 12 blocks of one device no regime appears more than 2 times, and some device names some regime exactly 2 times.
All inputs are finite; a program needn't handle non-finite values.
Results may differ from a plain program's by a relative error of at most 0.015.
Values may be sent and summed in bfloat16 or wider, within the bound.
No kernel may reach another device: no remote copies, remote signals or barrier semaphores. Data moves between devices by JAX's collectives and lax.ppermute only.
A program may use at most 128 MiB of HBM per device.

v0:
```python
import math

import jax
import jax.numpy as jnp
from jax import lax
from jax.sharding import PartitionSpec as P

NLAT = 640
NLON = 1280
BC = 16


def with_halo(array, sides, width):
    for axis, dim in sides:
        count, length = (lax.axis_size(axis), array.shape[dim])
        up = [(i, (i + 1) % count) for i in range(count)]
        down = [(j, i) for i, j in up]
        last = lax.slice_in_dim(array, length - width, length, axis=dim)
        leading = lax.slice_in_dim(array, 0, width, axis=dim)
        before = lax.ppermute(last, axis, up)
        after = lax.ppermute(leading, axis, down)
        array = jnp.concatenate([before, array, after], axis=dim)
    return array


def latitude_table(degrees, latitudes):
    degree_grid = lax.broadcasted_iota(jnp.int32, (degrees, latitudes), 0)
    row_index = lax.broadcasted_iota(jnp.int32, (degrees, latitudes), 1)
    phase_count = degree_grid * (2 * row_index + 1) % (4 * latitudes)
    phase_angle = phase_count.astype(jnp.float32) * (math.pi / (2.0 * latitudes))
    return (jnp.cos(phase_angle) * math.sqrt(2.0 / degrees)).astype(jnp.bfloat16)


def longitude_table(zonal_waves, longitudes):
    total_count = zonal_waves.shape[0]
    column_index = lax.broadcasted_iota(jnp.int32, (total_count, longitudes), 1)
    phase_count = zonal_waves[:, None] * column_index % longitudes
    phase_angle = phase_count.astype(jnp.float32) * (2.0 * math.pi / longitudes)
    scaling = 1.0 / math.sqrt(total_count)
    return jnp.stack(
        [jnp.cos(phase_angle) * scaling, -jnp.sin(phase_angle) * scaling], axis=1
    ).astype(jnp.bfloat16)


def damped(spectral, zonal_waves, strength, degrees):
    degree_grid = lax.broadcasted_iota(jnp.int32, spectral.shape, 3)
    component = lax.broadcasted_iota(jnp.int32, spectral.shape, 1)
    zonal_order = zonal_waves[:, None, None, None]
    retained = (degree_grid >= zonal_order) & ((component == 0) | (zonal_order > 0))
    relative = (degree_grid * (degree_grid + 1)).astype(jnp.float32) / float(
        degrees * (degrees + 1)
    )
    factor = 1.0 / (1.0 + strength[None, None, :, None] * relative * relative)
    return jnp.where(retained, spectral.astype(jnp.float32) * factor, 0.0).astype(jnp.bfloat16)


def transport(padded, zonal, meridional):
    centre = padded[1:-1, 1:-1]
    northern = padded[2:, 1:-1]
    southern = padded[:-2, 1:-1]
    eastern = padded[1:-1, 2:]
    western = padded[1:-1, :-2]
    along = (
        centre
        - 0.5 * zonal * (eastern - western)
        + 0.5 * zonal * zonal * (eastern - 2.0 * centre + western)
    )
    return (
        along
        - 0.5 * meridional * (northern - southern)
        + 0.5 * meridional * meridional * (northern - 2.0 * centre + southern)
    )


def clear_poles(padded, depth, lat_dim):
    position = lax.axis_index("lat")
    extent = padded.shape[lat_dim]
    lat_index = lax.broadcasted_iota(jnp.int32, padded.shape, lat_dim)
    lower_rim = (position == 0) & (lat_index < depth)
    upper_rim = (position == lax.axis_size("lat") - 1) & (lat_index >= extent - depth)
    return jnp.where(lower_rim | upper_rim, jnp.zeros_like(padded), padded)


def regime_net(columns, w_in, w_mid, w_out):
    layer_one = jax.nn.silu(
        jnp.einsum("abcl,lh->abch", columns, w_in, preferred_element_type=jnp.float32)
    ).astype(jnp.bfloat16)
    layer_two = jax.nn.silu(
        jnp.einsum("abch,hg->abcg", layer_one, w_mid, preferred_element_type=jnp.float32)
    ).astype(jnp.bfloat16)
    return jnp.einsum("abcg,gl->abcl", layer_two, w_out, preferred_element_type=jnp.float32).astype(
        jnp.bfloat16
    )


def body(
    spectral,
    wavenumber_of_slot,
    filter_strength,
    courant,
    sunlit_blocks,
    sunlit_owner,
    radiation_in,
    radiation_mid,
    radiation_out,
):
    own_count = spectral.shape[0]
    degrees = spectral.shape[3]
    own_waves = lax.dynamic_slice_in_dim(
        wavenumber_of_slot, lax.axis_index("lat") * own_count, own_count
    )
    filtered = damped(spectral, own_waves, filter_strength, degrees)
    coefficients = jnp.einsum(
        "scln,nj->sclj", filtered, latitude_table(degrees, NLAT), preferred_element_type=jnp.float32
    ).astype(jnp.bfloat16)
    wave_table = longitude_table(wavenumber_of_slot, NLON)
    level_slab = jnp.einsum(
        "sclj,sck->jkl",
        lax.all_to_all(coefficients, "lat", split_axis=3, concat_axis=0, tiled=True),
        wave_table,
        preferred_element_type=jnp.float32,
    ).astype(jnp.bfloat16)
    grid_field = lax.all_to_all(level_slab, "lon", split_axis=1, concat_axis=2, tiled=True)
    zonal = courant[0].astype(jnp.float32)
    meridional = courant[1].astype(jnp.float32)
    stacked = jnp.concatenate([grid_field[None], courant], axis=0)
    widened = clear_poles(with_halo(stacked, (("lat", 1), ("lon", 2)), 2), 2, 1)
    tracer = widened[0].astype(jnp.float32)
    wide_zonal = widened[1].astype(jnp.float32)
    wide_meridional = widened[2].astype(jnp.float32)
    tracer = transport(tracer, wide_zonal[1:-1, 1:-1], wide_meridional[1:-1, 1:-1])
    advected = transport(tracer, zonal, meridional)
    state = advected.astype(jnp.bfloat16)
    lat_rows, lon_cols, levels = state.shape
    owners = lax.axis_size("lon")
    blocks = state.reshape(lat_rows * (lon_cols // BC), BC * levels)
    sunlit = sunlit_blocks.reshape(-1)
    destination = sunlit_owner.reshape(-1)
    listed = sunlit.shape[0]
    picked = jnp.take(blocks, sunlit, axis=0)
    position_of = destination * listed + lax.iota(jnp.int32, listed)
    select = (
        position_of[:, None] == lax.broadcasted_iota(jnp.int32, (listed, owners * listed), 1)
    ).astype(jnp.bfloat16)
    outgoing = jnp.einsum("sp,sd->pd", select, picked, preferred_element_type=jnp.float32).astype(
        jnp.bfloat16
    )
    outgoing = outgoing.reshape(owners, listed, BC, levels)
    computed = regime_net(
        lax.all_to_all(outgoing, "lon", split_axis=0, concat_axis=0, tiled=True),
        radiation_in[0],
        radiation_mid[0],
        radiation_out[0],
    )
    returned = lax.all_to_all(computed, "lon", split_axis=0, concat_axis=0, tiled=True).reshape(
        owners * listed, BC * levels
    )
    own_rows = jnp.einsum("sp,pd->sd", select, returned, preferred_element_type=jnp.float32).astype(
        jnp.bfloat16
    )
    covering = (
        sunlit[:, None] == lax.broadcasted_iota(jnp.int32, (listed, blocks.shape[0]), 1)
    ).astype(jnp.bfloat16)
    heating = jnp.einsum(
        "sb,sd->bd", covering, own_rows, preferred_element_type=jnp.float32
    ).astype(jnp.bfloat16)
    return (advected, heating.reshape(lat_rows, lon_cols, levels))


def solution(mesh):
    in_specs = (
        P("lat", None, "lon", None),
        P(),
        P("lon"),
        P(None, "lat", "lon", None),
        P("lat", "lon", None),
        P("lat", "lon", None, None),
        P("lon", None, None),
        P("lon", None, None),
        P("lon", None, None),
    )
    out_specs = (P("lat", "lon", None), P("lat", "lon", None))
    return jax.shard_map(body, mesh=mesh, in_specs=in_specs, out_specs=out_specs, check_vma=False)
```

profile of v0, /device:TPU:0, one launch (start us, length us, event | category | flops | bytes accessed | tf_op | source)
XLA Modules:
  0.0 682.8 jit_solution(11425578820030568332)
XLA Ops:
  2.2 17.1 %convolution_convert_fusion.1 = bf16[160,2,16,640]{3,2,1,0:T(8,128)(2,1)} fusion(bf16[160,2,16,640]{3,2,1,0:T(8,128)(2,1)} %param.9, f32[640]{0:T(1024)S(1)} %broadcast_multiply_fusion, f32[16]{0:T(128)S(1)} %broadcast_multiply_fusion.1, f32[640]{0:T(1024)S(1)} %get-tuple-element.15, s32[160]{0:T(256)S(1)} %get-tuple-element.5, ...), kind=kOutput, calls=%fused_computation.32 | convolution fusion | flops 4238131200 | bytes 13115746 | tf_op jit(solution)/shard_map/scln,nj->sclj/dot_general | solution.py:113
  19.3 17.3 %copy.21 = bf16[160,2,16,640]{0,2,1,3:T(8,128)(2,1)} copy(bf16[160,2,16,640]{3,2,1,0:T(8,128)(2,1)} %convolution_convert_fusion.1) | data formatting | bytes 13107200 | tf_op jit(solution)/shard_map/convert_element_type | solution.py:115
  36.6 6.5 all-to-all-start
  43.1 15.8 %multiply_convert_fusion.1 = (bf16[640,1,1280]{2,0,1:T(8,128)(2,1)S(1)}, bf16[640,1,1280]{2,0,1:T(8,128)(2,1)}) fusion(s32[640]{0:T(1024)S(1)} %copy-done.1), kind=kLoop, calls=%fused_computation.49 | loop fusion | flops 11468800 | bytes 3279360 | tf_op jit(solution)/shard_map/convert.7
  58.8 213.6 %all-to-all-done = bf16[160,2,16,640]{0,2,1,3:T(8,128)(2,1)} async-done(((bf16[160,2,16,640]{0,2,1,3:T(8,128)(2,1)}), bf16[160,2,16,640]{0,2,1,3:T(8,128)(2,1)}, u32[]{:S(2)}, u32[]{:S(2)}) %all-to-all-start) | async-done | bytes 6553632 | tf_op jit(solution)/shard_map/all_to_all | solution.py:119
  272.4 14.7 %copy.39 = bf16[160,2,16,4,160]{0,3,4,1,2:T(4,128)(2,1)} copy(bf16[160,2,16,4,160]{0,2,1,4,3:T(8,128)(2,1)} %bitcast.2) | data formatting | bytes 13107200 | tf_op jit(solution)/shard_map/all_to_all | solution.py:119
  287.1 15.2 %all_to_all.33 = bf16[640,2,16,160]{0,3,1,2:T(8,128)(2,1)} reshape(bf16[4,160,2,16,160]{1,0,4,2,3:T(4,128)(2,1)} %bitcast.86) | data formatting | bytes 13107200 | tf_op jit(solution)/shard_map/all_to_all | solution.py:119
  302.4 13.0 %fusion.22 = bf16[160,1280,16]{1,0,2:T(8,128)(2,1)} fusion(bf16[640,2,16,160]{0,3,1,2:T(8,128)(2,1)} %all_to_all.33, bf16[640,1,1280]{2,0,1:T(8,128)(2,1)} %get-tuple-element.14, bf16[640,1,1280]{2,0,1:T(8,128)(2,1)S(1)} %get-tuple-element.13), kind=kOutput, calls=%fused_computation.42 | convolution fusion | flops 8398438400 | bytes 16384000 | tf_op jit(solution)/shard_map/sclj,sck->jkl/dot_general | solution.py:117
  315.3 16.1 %copy.23 = bf16[160,1280,16]{0,2,1:T(8,128)(2,1)} copy(bf16[160,1280,16]{1,0,2:T(8,128)(2,1)} %fusion.22) | data formatting | bytes 13107200 | tf_op jit(solution)/shard_map/convert_element_type | solution.py:122
  331.5 5.3 all-to-all-start.1
  336.8 116.5 %all-to-all-done.1 = bf16[160,1280,16]{0,2,1:T(8,128)(2,1)} async-done(((bf16[160,1280,16]{0,2,1:T(8,128)(2,1)}), bf16[160,1280,16]{0,2,1:T(8,128)(2,1)}, u32[]{:S(2)}, u32[]{:S(2)}) %all-to-all-start.1) | async-done | bytes 6553632 | tf_op jit(solution)/shard_map/all_to_all | solution.py:123
  453.3 19.5 %copy.24 = bf16[160,8,160,16]{2,3,1,0:T(8,128)(2,1)} copy(bf16[160,8,160,16]{0,3,2,1:T(8,128)(2,1)} %bitcast.9) | data formatting | bytes 13107200 | tf_op jit(solution)/shard_map/all_to_all | solution.py:123
  472.8 11.6 %copy.25 = bf16[1,160,160,128]{3,2,1,0:T(8,128)(2,1)} copy(bf16[1,160,160,128]{2,3,1,0:T(8,128)(2,1)} %bitcast.87) | data formatting | bytes 13107200 | tf_op jit(solution)/shard_map/broadcast_in_dim | solution.py:126
  489.4 5.5 collective-permute-done
  506.3 27.0 %maximum_select_fusion = bf16[3,164,164,128]{3,2,1,0:T(8,128)(2,1)} fusion(bf16[3,164,2,128]{3,2,1,0:T(2,128)(2,1)S(1)} %collective-permute-done.3, bf16[3,2,160,128]{3,2,1,0:T(8,128)(2,1)S(1)} %collective-permute-done.1, bf16[2,160,160,128]{3,2,1,0:T(8,128)(2,1)} %param.12, bf16[1,160,160,128]{3,2,1,0:T(8,128)(2,1)} %copy.25, ...), kind=kLoop, calls=%fused_computation.1 | loop fusion | flops 134264832 | bytes 41312420 | tf_op jit(solution)/shard_map/jit(_where)/select_n | solution.py:81
  533.2 16.4 %slice_bitcast_fusion.1 = (bf16[164,164,128]{2,1,0:T(8,128)(2,1)}, bf16[164,164,128]{2,1,0:T(8,128)(2,1)}, f32[164,164,128]{2,1,0:T(8,128)}) fusion(bf16[3,164,164,128]{3,2,1,0:T(8,128)(2,1)} %maximum_select_fusion), kind=kLoop, calls=%fused_computation.29 | loop fusion | flops 3442688 | bytes 48197632 | tf_op jit(solution)/shard_map/convert_element_type | solution.py:129
  549.7 40.2 %fusion.3 = f32[162,162,128]{2,1,0:T(8,128)} fusion(f32[164,164,128]{2,1,0:T(8,128)} %get-tuple-element.8, bf16[164,164,128]{2,1,0:T(8,128)(2,1)} %get-tuple-element.7, bf16[164,164,128]{2,1,0:T(8,128)(2,1)} %get-tuple-element.6), kind=kLoop, calls=%fused_computation.13 | loop fusion | flops 70543872 | bytes 94058496 | tf_op jit(solution)/shard_map/add | solution.py:69
  589.8 35.8 %fusion.74 = (bf16[160,160,128]{2,1,0:T(8,128)(2,1)}, f32[160,160,128]{2,1,0:T(8,128)}) fusion(f32[162,162,128]{2,1,0:T(8,128)} %fusion.3, bf16[2,160,160,128]{3,2,1,0:T(8,128)(2,1)} %param.12), kind=kLoop, calls=%fused_computation.119 | loop fusion | flops 72089600 | bytes 98304000 | tf_op jit(solution)/shard_map/convert_element_type | solution.py:133
  625.6 11.2 %reshape.162 = bf16[1600,2048]{1,0:T(8,128)(2,1)} reshape(bf16[160,160,128]{2,1,0:T(8,128)(2,1)} %get-tuple-element.2) | data formatting | bytes 13107200 | tf_op jit(solution)/shard_map/reshape | solution.py:136
  636.9 4.4 gather_fusion
  641.7 12.3 %all_to_all.43 = bf16[8,12,16,128]{3,2,1,0:T(8,128)(2,1)S(1)} all-to-all(bf16[8,12,16,128]{3,2,1,0:T(8,128)(2,1)S(1)} %bitcast.89), channel_id=1, replica_groups=mesh['lat'=4,'lon'=8] {'lon'}, dimensions={0} | all-to-all | bytes 786432 | tf_op jit(solution)/shard_map/all_to_all | solution.py:150
  656.6 10.7 %all_to_all.44 = bf16[8,12,16,128]{3,2,1,0:T(8,128)(2,1)S(1)} all-to-all(bf16[8,12,16,128]{3,2,1,0:T(8,128)(2,1)S(1)} %fusion.39), channel_id=1, replica_groups=mesh['lat'=4,'lon'=8] {'lon'}, dimensions={0} | all-to-all | bytes 786432 | tf_op jit(solution)/shard_map/all_to_all | solution.py:155
  667.3 4.2 convolution_convert_fusion
  671.5 11.1 %reshape.166 = bf16[160,160,128]{2,1,0:T(8,128)(2,1)} reshape(bf16[1600,2048]{1,0:T(8,128)(2,1)} %convolution_convert_fusion) | data formatting | bytes 13107200 | tf_op jit(solution)/shard_map/reshape | solution.py:167
  (35 shorter events, 20.9 us)
Async XLA Ops:
  0.6 654.4 %copy-start = (bf16[1,512,512]{2,1,0:T(8,128)(2,1)S(1)}, bf16[1,512,512]{2,1,0:T(8,128)(2,1)}, u32[]{:S(2)}) copy-start(bf16[1,512,512]{2,1,0:T(8,128)(2,1)} %param.16) | copy-start | bytes 1572868
  36.6 6.5 copy-start.1
  36.6 235.8 %all-to-all-start = ((bf16[160,2,16,640]{0,2,1,3:T(8,128)(2,1)}), bf16[160,2,16,640]{0,2,1,3:T(8,128)(2,1)}, u32[]{:S(2)}, u32[]{:S(2)}) async-start(bf16[160,2,16,640]{0,2,1,3:T(8,128)(2,1)} %copy.21), calls=%async_computation | async-start | bytes 20971520 | tf_op jit(solution)/shard_map/all_to_all | solution.py:119
  331.5 5.3 copy-start.2
  331.5 121.8 %all-to-all-start.1 = ((bf16[160,1280,16]{0,2,1:T(8,128)(2,1)}), bf16[160,1280,16]{0,2,1:T(8,128)(2,1)}, u32[]{:S(2)}, u32[]{:S(2)}) async-start(bf16[160,1280,16]{0,2,1:T(8,128)(2,1)} %copy.23), calls=%async_computation.1 | async-start | bytes 20971520 | tf_op jit(solution)/shard_map/all_to_all | solution.py:123
  485.5 14.8 %copy-start.5 = (s32[1,1,12,1]{2,3,1,0:T(1,128)S(1)}, s32[1,1,12,1]{2,3,1,0:T(1,128)}, u32[]{:S(2)}) copy-start(s32[1,1,12,1]{2,3,1,0:T(1,128)} %param.14) | copy-start | bytes 148
  485.5 9.4 %collective-permute-start = (bf16[3,2,160,128]{3,2,1,0:T(8,128)(2,1)S(1)}, bf16[3,2,160,128]{3,2,1,0:T(8,128)(2,1)S(1)}, u32[]{:S(2)}, u32[]{:S(2)}) collective-permute-start(bf16[3,2,160,128]{3,2,1,0:T(8,128)(2,1)S(1)} %get-tuple-element.11), channel_id=1, source_target_pairs={{0,8},{8,16},{16,24},{24,0},{1,9},{9,17},{17,25},{25,1},{2,10},{10... | collective-permute-start | bytes 737288 | tf_op jit(solution)/shard_map/ppermute | solution.py:20
  485.6 10.1 %collective-permute-start.1 = (bf16[3,2,160,128]{3,2,1,0:T(8,128)(2,1)S(1)}, bf16[3,2,160,128]{3,2,1,0:T(8,128)(2,1)S(1)}, u32[]{:S(2)}, u32[]{:S(2)}) collective-permute-start(bf16[3,2,160,128]{3,2,1,0:T(8,128)(2,1)S(1)} %get-tuple-element.12), channel_id=1, source_target_pairs={{8,0},{16,8},{24,16},{0,24},{9,1},{17,9},{25,17},{1,25},{10,2},{18... | collective-permute-start | bytes 737288 | tf_op jit(solution)/shard_map/ppermute | solution.py:21
  497.5 6.6 collective-permute-start.2
  497.6 8.7 %collective-permute-start.3 = (bf16[3,164,2,128]{3,2,1,0:T(2,128)(2,1)S(1)}, bf16[3,164,2,128]{3,2,1,0:T(2,128)(2,1)S(1)}, u32[]{:S(2)}, u32[]{:S(2)}) collective-permute-start(bf16[3,164,2,128]{3,2,1,0:T(2,128)(2,1)S(1)} %get-tuple-element.10), channel_id=1, source_target_pairs={{1,0},{2,1},{3,2},{4,3},{5,4},{6,5},{7,6},{0,7},{9,8},{10,9},{11,1... | collective-permute-start | bytes 755720 | tf_op jit(solution)/shard_map/ppermute | solution.py:21
  625.6 28.4 %copy-start.3 = (bf16[1,128,512]{2,1,0:T(8,128)(2,1)S(1)}, bf16[1,128,512]{2,1,0:T(8,128)(2,1)}, u32[]{:S(2)}) copy-start(bf16[1,128,512]{2,1,0:T(8,128)(2,1)} %param.15) | copy-start | bytes 393220
  636.9 18.2 %copy-start.4 = (bf16[1,512,128]{2,1,0:T(8,128)(2,1)S(1)}, bf16[1,512,128]{2,1,0:T(8,128)(2,1)}, u32[]{:S(2)}) copy-start(bf16[1,512,128]{2,1,0:T(8,128)(2,1)} %param.17) | copy-start | bytes 393220
where the time goes:
time: 694 us; the launch traced here: 683 us
  waiting for transfers between devices  342 us (49%)
  other arithmetic  140 us (20%)
  local copies, waits for them, and re-layouts  121 us (17%)
  matrix products  37.2 us (5%)
  blocking collectives  23 us (3%)
  starting transfers between devices  18.3 us (3%)
    all_to_all x1, waiting for transfers between devices, body(): lax.all_to_all(coefficients, 'lat', split_axis=3, concat_axis=0, tiled=True)  214 us
    all_to_all x1, waiting for transfers between devices, body(): lax.all_to_all(level_slab, 'lon', split_axis=1, concat_axis=2, tiled=True)  116 us
    add x1, other arithmetic, transport(): along - 0.5 * meridional * (northern - southern)  40.2 us
    convert_element_type x1, other arithmetic, body(): state = advected.astype(jnp.bfloat16)  35.8 us
    all_to_all x2, local copies, waits for them, and re-layouts, body(): lax.all_to_all(coefficients, 'lat', split_axis=3, concat_axis=0, tiled=True)  30 us
    select_n x1, other arithmetic, clear_poles(): return jnp.where(lower_rim | upper_rim, jnp.zeros_like(padded), padded)  27 us
    all_to_all x1, local copies, waits for them, and re-layouts, body(): lax.all_to_all(level_slab, 'lon', split_axis=1, concat_axis=2, tiled=True)  19.5 us
    convert_element_type x1, local copies, waits for them, and re-layouts, body(): coefficients = jnp.einsum('scln,nj->sclj', filtered, latitude_table(degre...  17.3 us
  transfers between devices with their start and end apart: 6, of which 6 were waited for; matrix products, arithmetic and copies ran while one was open for 2% of the time, Pallas kernels for 0%

commit v1 on v0

--- a/solution.py
+++ b/solution.py
@@ -1,13 +1,485 @@
+import functools
 import math
 
 import jax
 import jax.numpy as jnp
+import ml_dtypes
+import numpy as np
 from jax import lax
+from jax.experimental import pallas as pl
+from jax.experimental.pallas import tpu as pltpu
 from jax.sharding import PartitionSpec as P
 
-NLAT = 640
-NLON = 1280
 BC = 16
+CAP = 2
+LANES = 128
+PAIR = 64
+ROWS = 4
+EDGE = 2
+MAIN = 256
+REM = LANES + 2 * LANES
+
+F32 = jnp.float32
+BF16 = jnp.bfloat16
+
+
+def last_dims(lhs, rhs):
+    return lax.dot_general(lhs, rhs, (((1,), (1,)), ((), ())), preferred_element_type=F32)
+
+
+def latitude_rows(degrees, latitudes, bands):
+    band = latitudes // bands
+    first = np.arange(bands)[:, None] * band - EDGE
+    rows = first + np.arange(band + 2 * EDGE)[None, :]
+    phase = (np.arange(degrees)[None, None, :] * (2 * rows[:, :, None] + 1)) % (4 * latitudes)
+    table = np.cos(phase * (math.pi / (2.0 * latitudes))) * math.sqrt(2.0 / degrees)
+    inside = (rows >= 0) & (rows < latitudes)
+    return np.where(inside[:, :, None], table, 0.0).astype(ml_dtypes.bfloat16)
+
+
+def longitude_columns(waves, sources, longitudes, owners, group):
+    total = waves.shape[0]
+    width = longitudes // owners
+    per_source = jnp.broadcast_to(
+        waves.reshape(sources, total // sources, 1), (sources, total // sources, 2)
+    ).reshape(sources, -1)
+    rest = per_source[:, MAIN:]
+    row_wave = jnp.concatenate([per_source[:, :MAIN], rest, rest], axis=1).reshape(-1)
+    quarter = (jnp.arange(row_wave.shape[0], dtype=jnp.int32) % 2) * (longitudes // 4)
+    first = np.arange(owners)[:, None] * width - EDGE
+    main = (first + np.arange(LANES)[None, :]).reshape(owners // group, group * LANES)
+    rest_columns = (first + LANES + np.arange(PAIR)[None, :]).reshape(owners // group, group * PAIR)
+    columns = np.concatenate([main, rest_columns], axis=1) % longitudes
+    shape = (owners // group, row_wave.shape[0], columns.shape[1])
+    phase = (row_wave[None, :, None] * jnp.asarray(columns, jnp.int32)[:, None, :]) + quarter[None, :, None]
+    phase = jnp.broadcast_to(phase, shape) % longitudes
+    angle = phase.astype(F32) * (2.0 * math.pi / longitudes)
+    return (jnp.cos(angle) * (1.0 / math.sqrt(total))).astype(BF16)
+
+
+def regroup_kernel(waves_ref, x_ref, factor_ref, out_ref, scratch):
+    slots, _, levels, degrees = x_ref.shape
+    start = pl.program_id(0) * slots
+    degree = lax.broadcasted_iota(jnp.int32, (levels, degrees), 1)
+    factor = factor_ref[...]
+    for s in range(slots):
+        m = waves_ref[start + s]
+        for c in range(2):
+            least = m if c == 0 else jnp.where(m == 0, degrees, m)
+            value = x_ref[s, c].astype(F32) * factor
+            value = jnp.where(degree >= least, value, 0.0)
+            for n in range(degrees // LANES):
+                scratch[n, pl.ds((s * 2 + c) * levels, levels), :] = value[:, n * LANES : (n + 1) * LANES]
+    for l in range(levels):
+        for n in range(degrees // LANES):
+            part = scratch[n, pl.ds(l, slots * 2, stride=levels), :]
+            out_ref[l, :, n * LANES : (n + 1) * LANES] = part.astype(BF16)
+
+
+def regroup(spectral, own_waves, factor):
+    slots, parts, levels, degrees = spectral.shape
+    block = slots // 5
+    return pl.pallas_call(
+        regroup_kernel,
+        grid_spec=pltpu.PrefetchScalarGridSpec(
+            num_scalar_prefetch=1,
+            grid=(slots // block,),
+            in_specs=[
+                pl.BlockSpec((block, parts, levels, degrees), lambda i, w: (i, 0, 0, 0)),
+                pl.BlockSpec((levels, degrees), lambda i, w: (0, 0)),
+            ],
+            out_specs=pl.BlockSpec((levels, block * parts, degrees), lambda i, w: (0, i, 0)),
+            scratch_shapes=[pltpu.VMEM((degrees // LANES, block * parts * levels, LANES), F32)],
+        ),
+        out_shape=jax.ShapeDtypeStruct((levels, slots * parts, degrees), BF16),
+        name="regroup",
+    )(own_waves, spectral, factor)
+
+
+def latitude_kernel(p_ref, b_ref, out_ref, low, high, rest):
+    t = pl.program_id(0)
+    half = pl.num_programs(0)
+    bands = out_ref.shape[0]
+    count = p_ref.shape[0]
+    rows = count // bands
+    table = p_ref[...]
+    for h in range(2):
+        result = last_dims(table, b_ref[h, 0, :MAIN, :])
+        low[pl.ds(h * 8 + t, count, stride=16), :] = result[:, :LANES]
+        high[pl.ds(h * 8 + t, count, stride=16), :] = result[:, LANES:]
+    packed = jnp.concatenate([b_ref[0, 0, MAIN:, :], b_ref[1, 0, MAIN:, :]], axis=0)
+    rest[pl.ds(t, count, stride=8), :] = last_dims(table, packed)
+
+    @pl.when(t == half - 1)
+    def _():
+        for d in range(bands):
+            out_ref[d, : rows * 16] = low[d * rows * 16 : (d + 1) * rows * 16].astype(BF16)
+            out_ref[d, rows * 16 : rows * 32] = high[d * rows * 16 : (d + 1) * rows * 16].astype(BF16)
+            out_ref[d, rows * 32 :] = rest[d * rows * 8 : (d + 1) * rows * 8].astype(BF16)
+
+
+def latitude_transform(table, grouped, bands):
+    count, degrees = table.shape
+    levels, lanes, _ = grouped.shape
+    half = levels // 2
+    rows = count // bands
+    split = grouped.reshape(2, half, lanes, degrees)
+    return pl.pallas_call(
+        latitude_kernel,
+        grid=(half,),
+        in_specs=[
+            pl.BlockSpec((count, degrees), lambda t: (0, 0)),
+            pl.BlockSpec((2, 1, lanes, degrees), lambda t: (0, t, 0, 0)),
+        ],
+        out_specs=pl.BlockSpec((bands, rows * 40, LANES), lambda t: (0, 0, 0)),
+        out_shape=jax.ShapeDtypeStruct((bands, rows * 40, LANES), BF16),
+        scratch_shapes=[
+            pltpu.VMEM((count * 16, LANES), F32),
+            pltpu.VMEM((count * 16, LANES), F32),
+            pltpu.VMEM((count * 8, LANES), F32),
+        ],
+        name="latitude",
+    )(table, split)
+
+
+def longitude_kernel(r_ref, e_ref, out_ref, lhs):
+    sources = r_ref.shape[0]
+    rows = r_ref.shape[1] // 40
+    group = out_ref.shape[0]
+
+    @pl.when(pl.program_id(0) == 0)
+    def _():
+        lane = lax.broadcasted_iota(jnp.int32, (rows, 8, LANES), 2)
+        for a in range(sources):
+            at = a * REM
+            lhs[:, at : at + LANES] = r_ref[a, : rows * 16]
+            lhs[:, at + LANES : at + MAIN] = r_ref[a, rows * 16 : rows * 32]
+            rest = r_ref[a, rows * 32 :].astype(F32).reshape(rows, 8, LANES)
+            lower = jnp.where(lane < PAIR, rest, 0.0)
+            upper = jnp.where(lane < PAIR, 0.0, rest)
+            both = jnp.concatenate([lower, upper], axis=1).reshape(rows * 16, LANES)
+            lhs[:, at + MAIN : at + REM] = both.astype(BF16)
+
+    result = jnp.dot(lhs[...], e_ref[0], preferred_element_type=F32)
+    for i in range(group):
+        out_ref[i, : rows * 16] = result[:, i * LANES : (i + 1) * LANES].astype(BF16)
+    lane = lax.broadcasted_iota(jnp.int32, (rows * 8, LANES), 1)
+    for i in range(group // 2):
+        at = group * LANES + i * LANES
+        pairs = result[:, at : at + LANES].reshape(rows // 2, 2, 16, LANES)
+        even = pairs[:, 0].reshape(rows * 8, LANES)
+        odd = pairs[:, 1].reshape(rows * 8, LANES)
+        turned_even = pltpu.roll(even, PAIR, 1)
+        turned_odd = pltpu.roll(odd, PAIR, 1)
+        out_ref[2 * i, rows * 16 :] = jnp.where(lane < PAIR, even, turned_odd).astype(BF16)
+        out_ref[2 * i + 1, rows * 16 :] = jnp.where(lane < PAIR, turned_even, odd).astype(BF16)
+
+
+def longitude_transform(received, table, owners):
+    sources, length, _ = received.shape
+    rows = length // 40
+    parts, depth, width = table.shape
+    group = owners // parts
+    return pl.pallas_call(
+        longitude_kernel,
+        grid=(parts,),
+        in_specs=[
+            pl.BlockSpec((sources, length, LANES), lambda t: (0, 0, 0)),
+            pl.BlockSpec((1, depth, width), lambda t: (t, 0, 0)),
+        ],
+        out_specs=pl.BlockSpec((group, rows * 24, LANES), lambda t: (t, 0, 0)),
+        out_shape=jax.ShapeDtypeStruct((owners, rows * 24, LANES), BF16),
+        scratch_shapes=[pltpu.VMEM((rows * 16, depth), BF16)],
+        name="longitude",
+    )(received, table)
+
+
+def moved(centre, east, west, north, south, u, v):
+    twice = 2.0 * centre
+    along = (0.5 * u) * (u * ((east + west) - twice) - (east - west))
+    across = (0.5 * v) * (v * ((north + south) - twice) - (north - south))
+    return centre + (along + across)
+
+
+def transport_kernel(first, *refs):
+    if first:
+        main_ref, rest_ref, uv_ref, out_ref, q, uv, s = refs
+    else:
+        main_ref, rest_ref, uv_ref, old_main, old_rest, _, out_ref, q, uv, s = refs
+    t = pl.program_id(0)
+    base = (t % 2) * ROWS
+    prior = ROWS - base
+    out_cols = out_ref.shape[1]
+    wide = uv_ref.shape[2]
+    eye_row = lax.broadcasted_iota(jnp.int32, (LANES, LANES), 0)
+    eye_col = lax.broadcasted_iota(jnp.int32, (LANES, LANES), 1)
+    eye = jnp.where(eye_row == eye_col, 1.0, 0.0).astype(BF16)
+
+    def unpack(main, rest):
+        for r in range(ROWS // 2):
+            for j in (2 * r, 2 * r + 1):
+                tile = main[:, j * 16 : (j + 1) * 16, :].reshape(LANES, LANES)
+                q[base + j, :LANES, :] = last_dims(eye, tile)
+            tile = rest[:, r * 16 : (r + 1) * 16, :].reshape(LANES, LANES)
+            turned = last_dims(eye, tile)
+            q[base + 2 * r, LANES : LANES + PAIR, :] = turned[:PAIR]
+            q[base + 2 * r + 1, LANES : LANES + PAIR, :] = turned[PAIR:]
+
+    if first:
+        unpack(main_ref, rest_ref)
+    else:
+
+        @pl.when(t == 0)
+        def _():
+            unpack(old_main, old_rest)
+
+        @pl.when(t > 0)
+        def _():
+            unpack(main_ref, rest_ref)
+
+    for i in range(ROWS):
+        for k in range(2):
+            uv[k, base + i] = uv_ref[k, i].astype(F32)
+
+    def at(i):
+        return base + i if i >= 0 else prior + ROWS + i
+
+    step = 24
+    for i in range(-1, ROWS - 1):
+        for o in range(0, wide, step):
+            s[at(i), pl.ds(o, step), :] = moved(
+                q[at(i), pl.ds(o + 1, step), :],
+                q[at(i), pl.ds(o + 2, step), :],
+                q[at(i), pl.ds(o, step), :],
+                q[at(i + 1), pl.ds(o + 1, step), :],
+                q[at(i - 1), pl.ds(o + 1, step), :],
+                uv[0, at(i), pl.ds(o, step), :],
+                uv[1, at(i), pl.ds(o, step), :],
+            )
+    step = 32
+    for i in range(-2, ROWS - 2):
+        for o in range(0, out_cols, step):
+            out_ref[i + 2, pl.ds(o, step), :] = moved(
+                s[at(i), pl.ds(o + 1, step), :],
+                s[at(i), pl.ds(o + 2, step), :],
+                s[at(i), pl.ds(o, step), :],
+                s[at(i + 1), pl.ds(o + 1, step), :],
+                s[at(i - 1), pl.ds(o + 1, step), :],
+                uv[0, at(i), pl.ds(o + 1, step), :],
+                uv[1, at(i), pl.ds(o + 1, step), :],
+            )
+
+
+def transport(fields, index, starts, courant, advected, shape):
+    field = fields[index]
+    owners, length, _ = field.shape
+    rows = length // 24
+    blocks = rows // ROWS
+    offset = starts[index] // ROWS
+    first = index == 0
+    wide = courant.shape[2]
+    lead = 0 if first else 1
+    main = (owners, ROWS * 16, LANES)
+    rest = (owners, ROWS * 8, LANES)
+
+    def rest_at(count):
+        return count * ROWS * 16 // (ROWS * 8)
+
+    in_specs = [
+        pl.BlockSpec(main, lambda t: (0, jnp.maximum(t - lead, 0), 0)),
+        pl.BlockSpec(rest, lambda t: (0, rest_at(blocks) + jnp.maximum(t - lead, 0), 0)),
+        pl.BlockSpec((2, ROWS, wide, LANES), lambda t: (0, offset + t - lead, 0, 0)),
+    ]
+    operands = [field, field, courant]
+    aliases = {}
+    if not first:
+        old = fields[index - 1]
+        old_blocks = old.shape[1] // 24 // ROWS
+        in_specs += [
+            pl.BlockSpec(main, lambda t: (0, old_blocks - 1, 0)),
+            pl.BlockSpec(rest, lambda t: (0, rest_at(old_blocks) + old_blocks - 1, 0)),
+            pl.BlockSpec(memory_space=pl.ANY),
+        ]
+        operands += [old, old, advected]
+        aliases = {5: 0}
+    return pl.pallas_call(
+        functools.partial(transport_kernel, first),
+        grid=(blocks + lead,),
+        in_specs=in_specs,
+        out_specs=pl.BlockSpec(
+            (ROWS,) + shape[1:], lambda t: (jnp.maximum(t, 1) - 1 + offset - lead, 0, 0)
+        ),
+        out_shape=jax.ShapeDtypeStruct(shape, F32),
+        scratch_shapes=[
+            pltpu.VMEM((2 * ROWS, LANES + PAIR, LANES), F32),
+            pltpu.VMEM((2, 2 * ROWS, wide, LANES), F32),
+            pltpu.VMEM((2 * ROWS, wide, LANES), F32),
+        ],
+        input_output_aliases=aliases,
+        name="transport",
+    )(*operands)
+
+
+def gather_kernel(blocks_ref, places_ref, state_ref, out_ref):
+    t = pl.program_id(0)
+
+    @pl.when(t == 0)
+    def _():
+        out_ref[...] = jnp.zeros_like(out_ref)
+
+    at = pl.multiple_of(places_ref[t] * BC, BC)
+    out_ref[pl.ds(at, BC), :] = state_ref[0].astype(BF16)
+
+
+def gather_blocks(advected, blocks, places, owners):
+    lon_cols, levels = advected.shape[1:]
+    across = lon_cols // BC
+    return pl.pallas_call(
+        gather_kernel,
+        grid_spec=pltpu.PrefetchScalarGridSpec(
+            num_scalar_prefetch=2,
+            grid=(blocks.shape[0],),
+            in_specs=[
+                pl.BlockSpec((1, BC, levels), lambda t, b, p: (b[t] // across, b[t] % across, 0))
+            ],
+            out_specs=pl.BlockSpec((owners * CAP * BC, levels), lambda t, b, p: (0, 0)),
+        ),
+        out_shape=jax.ShapeDtypeStruct((owners * CAP * BC, levels), BF16),
+        name="gather_blocks",
+    )(blocks, places, advected)
+
+
+def network_kernel(x_ref, in_ref, mid_ref, out_ref, y_ref):
+    def silu(v):
+        return (v / (1.0 + jnp.exp(-v))).astype(BF16)
+
+    one = silu(jnp.dot(x_ref[...], in_ref[...], preferred_element_type=F32))
+    two = silu(jnp.dot(one, mid_ref[...], preferred_element_type=F32))
+    y_ref[...] = jnp.dot(two, out_ref[...], preferred_element_type=F32).astype(BF16)
+
+
+def network(columns, w_in, w_mid, w_out):
+    return pl.pallas_call(
+        network_kernel,
+        out_shape=jax.ShapeDtypeStruct((columns.shape[0], w_out.shape[1]), BF16),
+        name="network",
+    )(columns, w_in, w_mid, w_out)
+
+
+def scatter_kernel(blocks_ref, places_ref, rows_ref, _, out_ref):
+    at = pl.multiple_of(places_ref[pl.program_id(0)] * BC, BC)
+    out_ref[0] = rows_ref[pl.ds(at, BC), :]
+
+
+def scatter_blocks(rows, blocks, places, empty):
+    levels = empty.shape[2]
+    across = empty.shape[1] // BC
+    return pl.pallas_call(
+        scatter_kernel,
+        grid_spec=pltpu.PrefetchScalarGridSpec(
+            num_scalar_prefetch=2,
+            grid=(blocks.shape[0],),
+            in_specs=[
+                pl.BlockSpec(rows.shape, lambda t, b, p: (0, 0)),
+                pl.BlockSpec(memory_space=pl.ANY),
+            ],
+            out_specs=pl.BlockSpec(
+                (1, BC, levels), lambda t, b, p: (b[t] // across, b[t] % across, 0)
+            ),
+        ),
+        out_shape=jax.ShapeDtypeStruct(empty.shape, BF16),
+        input_output_aliases={3: 0},
+        name="scatter_blocks",
+    )(blocks, places, rows, empty)
+
+
+def widened_courant(courant):
+    bands = lax.axis_size("lat")
+    owners = lax.axis_size("lon")
+    up = [(i, i + 1) for i in range(bands - 1)]
+    down = [(i + 1, i) for i in range(bands - 1)]
+    south = lax.ppermute(courant[:, -1:], "lat", up)
+    north = lax.ppermute(courant[:, :1], "lat", down)
+    tall = jnp.concatenate([south, courant, north], axis=1)
+    ahead = [(i, (i + 1) % owners) for i in range(owners)]
+    back = [(j, i) for i, j in ahead]
+    west = lax.ppermute(tall[:, :, -1:], "lon", ahead)
+    east = lax.ppermute(tall[:, :, :1], "lon", back)
+    wide = jnp.concatenate([west, tall, east], axis=2)
+    spare = -wide.shape[2] % 24
+    return jnp.pad(wide, ((0, 0), (1, 1), (0, spare), (0, 0)))
+
+
+def chunk_sizes(rows):
+    blocks = rows // ROWS
+    cuts = [round(blocks * f) for f in (0.0, 0.3, 0.58, 0.82)] + [blocks]
+    return [(b - a) * ROWS for a, b in zip(cuts, cuts[1:])]
+
+
+def tiled_body(
+    spectral,
+    wavenumber_of_slot,
+    filter_strength,
+    courant,
+    sunlit_blocks,
+    sunlit_owner,
+    radiation_in,
+    radiation_mid,
+    radiation_out,
+):
+    bands = lax.axis_size("lat")
+    owners = lax.axis_size("lon")
+    slots, parts, own_levels, degrees = spectral.shape
+    _, lat_rows, lon_cols, levels = courant.shape
+    latitudes = lat_rows * bands
+    longitudes = lon_cols * owners
+    own_waves = lax.dynamic_slice_in_dim(wavenumber_of_slot, lax.axis_index("lat") * slots, slots)
+    degree = jnp.arange(degrees, dtype=jnp.int32)
+    relative = (degree * (degree + 1)).astype(F32) / float(degrees * (degrees + 1))
+    factor = 1.0 / (1.0 + filter_strength[:, None] * relative[None, :] * relative[None, :])
+
+    rows = lat_rows + 2 * EDGE
+    sizes = chunk_sizes(rows)
+    starts = [sum(sizes[:i]) for i in range(len(sizes))]
+    lat_table = latitude_rows(degrees, latitudes, bands)
+    grouped = regroup(spectral, own_waves, factor)
+    received = []
+    for start, size in zip(starts, sizes):
+        piece = jnp.asarray(lat_table[:, start : start + size].reshape(bands * size, degrees))
+        sent = latitude_transform(piece, grouped, bands)
+        received.append(lax.all_to_all(sent, "lat", split_axis=0, concat_axis=0, tiled=True))
+
+    lon_table = longitude_columns(wavenumber_of_slot, bands, longitudes, owners, owners // 2)
+    wide = widened_courant(courant)
+    fields = []
+    for piece in received:
+        sent = longitude_transform(piece, lon_table, owners)
+        fields.append(lax.all_to_all(sent, "lon", split_axis=0, concat_axis=0, tiled=True))
+
+    advected = None
+    for index in range(len(fields)):
+        advected = transport(fields, index, starts, wide, advected, (lat_rows, lon_cols, levels))
+
+    blocks = sunlit_blocks.reshape(-1)
+    regime = sunlit_owner.reshape(-1)
+    listed = blocks.shape[0]
+    order = jnp.arange(listed, dtype=jnp.int32)
+    same = (regime[:, None] == regime[None, :]) & (order[None, :] < order[:, None])
+    places = regime * CAP + jnp.sum(same.astype(jnp.int32), axis=1)
+    picked = gather_blocks(advected, blocks, places, owners).reshape(owners, CAP * BC, levels)
+    arrived = lax.all_to_all(picked, "lon", split_axis=0, concat_axis=0, tiled=True)
+    computed = network(
+        arrived.reshape(owners * CAP * BC, levels),
+        radiation_in[0],
+        radiation_mid[0],
+        radiation_out[0],
+    ).reshape(owners, CAP * BC, levels)
+    returned = lax.all_to_all(computed, "lon", split_axis=0, concat_axis=0, tiled=True)
+    empty = jnp.zeros((lat_rows, lon_cols, levels), BF16)
+    heating = scatter_blocks(
+        returned.reshape(owners * CAP * BC, levels), blocks, places, empty
+    )
+    return (advected, heating)
 
 
 def with_halo(array, sides, width):
@@ -54,7 +526,7 @@
     return jnp.where(retained, spectral.astype(jnp.float32) * factor, 0.0).astype(jnp.bfloat16)
 
 
-def transport(padded, zonal, meridional):
+def plain_transport(padded, zonal, meridional):
     centre = padded[1:-1, 1:-1]
     northern = padded[2:, 1:-1]
     southern = padded[:-2, 1:-1]
@@ -93,7 +565,7 @@
     )
 
 
-def body(
+def plain_body(
     spectral,
     wavenumber_of_slot,
     filter_strength,
@@ -111,9 +583,9 @@
     )
     filtered = damped(spectral, own_waves, filter_strength, degrees)
     coefficients = jnp.einsum(
-        "scln,nj->sclj", filtered, latitude_table(degrees, NLAT), preferred_element_type=jnp.float32
-    ).astype(jnp.bfloat16)
-    wave_table = longitude_table(wavenumber_of_slot, NLON)
+        "scln,nj->sclj", filtered, latitude_table(degrees, courant.shape[1] * lax.axis_size("lat")), preferred_element_type=jnp.float32
+    ).astype(jnp.bfloat16)
+    wave_table = longitude_table(wavenumber_of_slot, courant.shape[2] * lax.axis_size("lon"))
     level_slab = jnp.einsum(
         "sclj,sck->jkl",
         lax.all_to_all(coefficients, "lat", split_axis=3, concat_axis=0, tiled=True),
@@ -128,8 +600,8 @@
     tracer = widened[0].astype(jnp.float32)
     wide_zonal = widened[1].astype(jnp.float32)
     wide_meridional = widened[2].astype(jnp.float32)
-    tracer = transport(tracer, wide_zonal[1:-1, 1:-1], wide_meridional[1:-1, 1:-1])
-    advected = transport(tracer, zonal, meridional)
+    tracer = plain_transport(tracer, wide_zonal[1:-1, 1:-1], wide_meridional[1:-1, 1:-1])
+    advected = plain_transport(tracer, zonal, meridional)
     state = advected.astype(jnp.bfloat16)
     lat_rows, lon_cols, levels = state.shape
     owners = lax.axis_size("lon")
@@ -167,6 +639,23 @@
     return (advected, heating.reshape(lat_rows, lon_cols, levels))
 
 
+def fits(spectral, courant, bands, owners):
+    total, parts, levels, degrees = spectral.shape
+    width = courant.shape[2] // owners
+    height = courant.shape[1] // bands
+    return (
+        parts == 2
+        and levels == LANES
+        and levels // owners == 16
+        and 2 * (total // bands) == MAIN + PAIR
+        and degrees % LANES == 0
+        and (total // bands) % 5 == 0
+        and height % ROWS == 0
+        and width % 32 == 0
+        and LANES < width + 2 * EDGE <= LANES + PAIR - 8
+    )
+
+
 def solution(mesh):
     in_specs = (
         P("lat", None, "lon", None),
@@ -180,4 +669,12 @@
         P("lon", None, None),
     )
     out_specs = (P("lat", "lon", None), P("lat", "lon", None))
-    return jax.shard_map(body, mesh=mesh, in_specs=in_specs, out_specs=out_specs, check_vma=False)
+    bands, owners = mesh.shape["lat"], mesh.shape["lon"]
+
+    def run(*arrays):
+        body = tiled_body if fits(arrays[0], arrays[3], bands, owners) else plain_body
+        return jax.shard_map(
+            body, mesh=mesh, in_specs=in_specs, out_specs=out_specs, check_vma=False
+        )(*arrays)
+
+    return run

time: 694 us -> 406 us (0.59); the launches traced: 683 us -> 402 us
  waiting for transfers between devices: 342 us -> 125 us
  Pallas kernels: 0 us -> 136 us
  local copies, waits for them, and re-layouts: 121 us -> 23.9 us
  other arithmetic: 140 us -> 58.8 us
  matrix products: 37.2 us -> 0 us
  starting transfers between devices: 18.3 us -> 40.2 us
    all_to_all x2 -> x8, waiting for transfers between devices: 330 us -> 124 us  [the longest x4 84.2 us: tiled_body(): lax.all_to_all(sent, 'lat', split_axis=0, concat_axis=0, tiled=True)]
    pallas_call x0 -> x16, Pallas kernels: none -> 136 us  [the longest x4 48.4 us: transport(): pl.pallas_call(functools.partial(transport_kernel, first), grid=(blocks +...]
    all_to_all x3 -> x0, local copies, waits for them, and re-layouts: 49.4 us -> none  [the longest x2 30 us: body(): lax.all_to_all(coefficients, 'lat', split_axis=3, concat_axis=0, tiled=True)]
    add x2 -> x1, other arithmetic: 40.2 us -> 0.51 us  [tiled_body(): places = regime * CAP + jnp.sum(same.astype(jnp.int32), axis=1)]
    dot_general x6 -> x0, matrix products: 37.2 us -> none  [the longest x1 17.1 us: body(): jnp.einsum('scln,nj->sclj', filtered, latitude_table(degrees, NLAT), pref...]
    convert_element_type x2 -> x0, local copies, waits for them, and re-layouts: 33.4 us -> none  [the longest x1 17.3 us: body(): coefficients = jnp.einsum('scln,nj->sclj', filtered, latitude_table(degre...]
    select_n x2 -> x0, other arithmetic: 27 us -> none  [the longest x1 27 us: clear_poles(): return jnp.where(lower_rim | upper_rim, jnp.zeros_like(padded), padded)]
    reshape x2 -> x1, local copies, waits for them, and re-layouts: 22.3 us -> 0.09 us  [longitude_columns(): per_source = jnp.broadcast_to(waves.reshape(sources, total // sources, 1)...]
  transfers between devices with their start and end apart: 6 -> 12, of which waited for: 6 -> 7; matrix products, arithmetic and copies ran while one was open for 2% -> 17% of each run, Pallas kernels for 0% -> 23%
where the time goes in v1:
time: 406 us; the launch traced here: 402 us
  Pallas kernels  136 us (33%)
  waiting for transfers between devices  125 us (31%)
  other arithmetic  58.8 us (14%)
  starting transfers between devices  40.2 us (10%)
  local copies, waits for them, and re-layouts  23.9 us (6%)
  blocking collectives  18.2 us (4%)
    all_to_all x4, waiting for transfers between devices, tiled_body(): lax.all_to_all(sent, 'lat', split_axis=0, concat_axis=0, tiled=True)  84.2 us
    pallas_call x4, Pallas kernels, transport(): pl.pallas_call(functools.partial(transport_kernel, first), grid=(blocks +...  48.4 us
    all_to_all x4, waiting for transfers between devices, tiled_body(): lax.all_to_all(sent, 'lon', split_axis=0, concat_axis=0, tiled=True)  39.8 us
    convert_element_type x1, other arithmetic, longitude_columns(): return (jnp.cos(angle) * (1.0 / math.sqrt(total))).astype(BF16)  39.2 us
    pallas_call x4, Pallas kernels, latitude_transform(): pl.pallas_call(latitude_kernel, grid=(half,), in_specs=[pl.BlockSpec((cou...  34.6 us
    pallas_call x4, Pallas kernels, longitude_transform(): pl.pallas_call(longitude_kernel, grid=(parts,), in_specs=[pl.BlockSpec((s...  28.4 us
    all_to_all x4, starting transfers between devices, tiled_body(): lax.all_to_all(sent, 'lat', split_axis=0, concat_axis=0, tiled=True)  17.9 us
    concatenate x1, other arithmetic, widened_courant(): wide = jnp.concatenate([west, tall, east], axis=2)  17.5 us
  transfers between devices with their start and end apart: 12, of which 7 were waited for; matrix products, arithmetic and copies ran while one was open for 17% of the time, Pallas kernels for 23%

profile of v1, /device:TPU:0, one launch (start us, length us, event | category | flops | bytes accessed | tf_op | source)
XLA Modules:
  0.0 402.5 jit_solution(15882120918959609210)
XLA Ops:
  3.3 11.1 %regroup.1 = bf16[16,320,640]{2,1,0:T(8,128)(2,1)} custom-call(s32[160]{0:T(256)} %dynamic_slice.3.waves_ref, bf16[160,2,16,640]{3,2,1,0:T(8,128)(2,1)} %x_ref.1, f32[16,640]{1,0:T(8,128)} %add_divide_fusion.factor_ref), custom_call_target="tpu_custom_call" | custom-call | tf_op jit(solution)/shard_map/regroup/pallas_call | solution.py:82
  14.5 8.2 %latitude.4 = bf16[4,1120,128]{2,1,0:T(8,128)(2,1)} custom-call(bf16[112,640]{1,0:T(8,128)(2,1)} %constant.66.clone.p_ref, bf16[2,8,320,640]{3,2,1,0:T(8,128)(2,1)} %bitcast.12), custom_call_target="tpu_custom_call" | custom-call | tf_op jit(solution)/shard_map/latitude/pallas_call | solution.py:127
  22.6 6.3 %all-to-all-start = ((bf16[4,1120,128]{2,1,0:T(8,128)(2,1)}), bf16[4,1120,128]{2,1,0:T(8,128)(2,1)S(1)}, u32[]{:S(2)}, u32[]{:S(2)}) async-start(bf16[4,1120,128]{2,1,0:T(8,128)(2,1)} %latitude.4), calls=%async_computation | async-start | bytes 2293760 | tf_op jit(solution)/shard_map/all_to_all | solution.py:450
  29.0 8.5 %latitude.5 = bf16[4,1600,128]{2,1,0:T(8,128)(2,1)} custom-call(bf16[160,640]{1,0:T(8,128)(2,1)} %constant.65.clone.p_ref, bf16[2,8,320,640]{3,2,1,0:T(8,128)(2,1)} %bitcast.13), custom_call_target="tpu_custom_call" | custom-call | tf_op jit(solution)/shard_map/latitude/pallas_call | solution.py:127
  37.5 19.3 %all-to-all-done.r_ref = bf16[4,1120,128]{2,1,0:T(8,128)(2,1)S(1)} async-done(((bf16[4,1120,128]{2,1,0:T(8,128)(2,1)}), bf16[4,1120,128]{2,1,0:T(8,128)(2,1)S(1)}, u32[]{:S(2)}, u32[]{:S(2)}) %all-to-all-start) | async-done | bytes 1146912 | tf_op jit(solution)/shard_map/all_to_all | solution.py:450
  60.4 8.9 %latitude.6 = bf16[4,1920,128]{2,1,0:T(8,128)(2,1)} custom-call(bf16[192,640]{1,0:T(8,128)(2,1)} %constant.64.clone.p_ref, bf16[2,8,320,640]{3,2,1,0:T(8,128)(2,1)} %bitcast.14), custom_call_target="tpu_custom_call" | custom-call | tf_op jit(solution)/shard_map/latitude/pallas_call | solution.py:127
  69.3 29.0 %all-to-all-done.2.r_ref = bf16[4,1600,128]{2,1,0:T(8,128)(2,1)S(1)} async-done(((bf16[4,1600,128]{2,1,0:T(8,128)(2,1)}), bf16[4,1600,128]{2,1,0:T(8,128)(2,1)S(1)}, u32[]{:S(2)}, u32[]{:S(2)}) %all-to-all-start.2) | async-done | bytes 1638432 | tf_op jit(solution)/shard_map/all_to_all | solution.py:450
  103.1 9.0 %latitude.7 = bf16[4,1920,128]{2,1,0:T(8,128)(2,1)} custom-call(bf16[192,640]{1,0:T(8,128)(2,1)} %constant.63.clone.p_ref, bf16[2,8,320,640]{3,2,1,0:T(8,128)(2,1)} %bitcast.15), custom_call_target="tpu_custom_call" | custom-call | tf_op jit(solution)/shard_map/latitude/pallas_call | solution.py:127
  112.1 35.9 %all-to-all-done.4.r_ref = bf16[4,1920,128]{2,1,0:T(8,128)(2,1)S(1)} async-done(((bf16[4,1920,128]{2,1,0:T(8,128)(2,1)}), bf16[4,1920,128]{2,1,0:T(8,128)(2,1)S(1)}, u32[]{:S(2)}, u32[]{:S(2)}) %all-to-all-start.4) | async-done | bytes 1966112 | tf_op jit(solution)/shard_map/all_to_all | solution.py:450
  153.0 39.2 %fusion.9.e_ref = bf16[2,1536,768]{2,1,0:T(8,128)(2,1)} fusion(s32[1536]{0:T(1024)S(1)} %fusion.13, s32[2,768]{1,0:T(2,128)S(1)} %copy-done.8, s32[1536]{0:T(1024)S(1)} %mul.79), kind=kLoop, calls=%fused_computation.15 | loop fusion | flops 28311552 | bytes 4737024 | tf_op jit(solution)/shard_map/convert_element_type | solution.py:57
  192.3 7.0 %longitude.5 = bf16[8,960,128]{2,1,0:T(8,128)(2,1)} custom-call(bf16[4,1600,128]{2,1,0:T(8,128)(2,1)} %copy-done.5, bf16[2,1536,768]{2,1,0:T(8,128)(2,1)} %fusion.9.e_ref), custom_call_target="tpu_custom_call" | custom-call | tf_op jit(solution)/shard_map/longitude/pallas_call | solution.py:183
  203.0 7.8 %longitude.6 = bf16[8,1152,128]{2,1,0:T(8,128)(2,1)} custom-call(bf16[4,1920,128]{2,1,0:T(8,128)(2,1)} %copy-done.4, bf16[2,1536,768]{2,1,0:T(8,128)(2,1)} %fusion.9.e_ref), custom_call_target="tpu_custom_call" | custom-call | tf_op jit(solution)/shard_map/longitude/pallas_call | solution.py:183
  210.9 17.4 %all-to-all-done.3.refs_0_.refs_1_.refs_3_.refs_4_ = bf16[8,960,128]{2,1,0:T(8,128)(2,1)S(1)} async-done(((bf16[8,960,128]{2,1,0:T(8,128)(2,1)}), bf16[8,960,128]{2,1,0:T(8,128)(2,1)S(1)}, u32[]{:S(2)}, u32[]{:S(2)}) %all-to-all-start.3) | async-done | bytes 1966112 | tf_op jit(solution)/shard_map/all_to_all | solution.py:457
  233.3 7.8 %longitude.7 = bf16[8,1152,128]{2,1,0:T(8,128)(2,1)} custom-call(bf16[4,1920,128]{2,1,0:T(8,128)(2,1)} %all-to-all-done.6.r_ref, bf16[2,1536,768]{2,1,0:T(8,128)(2,1)} %fusion.9.e_ref), custom_call_target="tpu_custom_call" | custom-call | tf_op jit(solution)/shard_map/longitude/pallas_call | solution.py:183
  241.1 21.3 %all-to-all-done.5.refs_0_.refs_1_.refs_3_.refs_4_ = bf16[8,1152,128]{2,1,0:T(8,128)(2,1)S(1)} async-done(((bf16[8,1152,128]{2,1,0:T(8,128)(2,1)}), bf16[8,1152,128]{2,1,0:T(8,128)(2,1)S(1)}, u32[]{:S(2)}, u32[]{:S(2)}) %all-to-all-start.5) | async-done | bytes 2359328 | tf_op jit(solution)/shard_map/all_to_all | solution.py:457
  273.9 8.9 %constant_dynamic-update-slice_fusion.1 = bf16[2,162,160,128]{3,2,1,0:T(8,128)(2,1)S(1)} fusion(bf16[2,162,160,128]{3,2,1,0:T(8,128)(2,1)S(1)} %constant_dynamic-update-slice_fusion.2, bf16[2,160,160,128]{3,2,1,0:T(8,128)(2,1)} %param.17), kind=kLoop, calls=%fused_computation.24 | loop fusion | bytes 26214400
  290.1 5.7 %longitude.4 = bf16[8,672,128]{2,1,0:T(8,128)(2,1)} custom-call(bf16[4,1120,128]{2,1,0:T(8,128)(2,1)} %copy-done.6, bf16[2,1536,768]{2,1,0:T(8,128)(2,1)} %fusion.9.e_ref), custom_call_target="tpu_custom_call" | custom-call | tf_op jit(solution)/shard_map/longitude/pallas_call | solution.py:183
  300.5 17.5 %select_maximum_fusion.refs_2_ = bf16[2,164,168,128]{3,2,1,0:T(8,128)(2,1)} fusion(bf16[2,162,1,128]{3,2,1,0:T(2,128)(2,1)S(1)} %collective-permute-done.3, bf16[2,162,160,128]{3,2,1,0:T(8,128)(2,1)} %copy-done.2, bf16[2,162,1,128]{3,2,1,0:T(2,128)(2,1)S(1)} %collective-permute-done.2), kind=kLoop, calls=%fused_computation.6 | loop fusion | flops 119906304 | bytes 27543552 | tf_op jit(solution)/shard_map/concatenate | solution.py:408
  318.0 13.0 %transport.4.refs_5_ = f32[160,160,128]{2,1,0:T(8,128)} custom-call(bf16[8,1152,128]{2,1,0:T(8,128)(2,1)} %all-to-all-done.7.refs_0_.refs_1_.refs_3_.refs_4_, bf16[8,1152,128]{2,1,0:T(8,128)(2,1)} %all-to-all-done.7.refs_0_.refs_1_.refs_3_.refs_4_, bf16[2,164,168,128]{3,2,1,0:T(8,128)(2,1)} %select_maximum_fusion.refs_2_), custom_call_target="tpu_custom_call" | custom-call | tf_op jit(solution)/shard_map/transport/pallas_call | solution.py:305
  331.0 14.1 %transport.5.refs_5_ = f32[160,160,128]{2,1,0:T(8,128)} custom-call(bf16[8,1152,128]{2,1,0:T(8,128)(2,1)} %copy-done, bf16[8,1152,128]{2,1,0:T(8,128)(2,1)} %copy-done, bf16[2,164,168,128]{3,2,1,0:T(8,128)(2,1)} %select_maximum_fusion.refs_2_, bf16[8,1152,128]{2,1,0:T(8,128)(2,1)} %all-to-all-done.7.refs_0_.refs_1_.refs_3_.refs_4_, ...), custom_call_target="tpu_custom_call", output_to_operand_aliasing={{}: (5, {})} | custom-call | tf_op jit(solution)/shard_map/transport/pallas_call | solution.py:305
  345.1 12.2 %transport.6.refs_5_ = f32[160,160,128]{2,1,0:T(8,128)} custom-call(bf16[8,960,128]{2,1,0:T(8,128)(2,1)} %copy-done.1, bf16[8,960,128]{2,1,0:T(8,128)(2,1)} %copy-done.1, bf16[2,164,168,128]{3,2,1,0:T(8,128)(2,1)} %select_maximum_fusion.refs_2_, bf16[8,1152,128]{2,1,0:T(8,128)(2,1)} %copy-done, ...), custom_call_target="tpu_custom_call", output_to_operand_aliasing={{}: (5, {})} | custom-call | tf_op jit(solution)/shard_map/transport/pallas_call | solution.py:305
  358.4 9.1 %transport.7.state_ref = f32[160,160,128]{2,1,0:T(8,128)} custom-call(bf16[8,672,128]{2,1,0:T(8,128)(2,1)} %copy-done.3, bf16[8,672,128]{2,1,0:T(8,128)(2,1)} %copy-done.3, bf16[2,164,168,128]{3,2,1,0:T(8,128)(2,1)} %select_maximum_fusion.refs_2_, bf16[8,960,128]{2,1,0:T(8,128)(2,1)} %copy-done.1, ...), custom_call_target="tpu_custom_call", output_to_operand_aliasing={{}: (5, {})} | custom-call | tf_op jit(solution)/shard_map/transport/pallas_call | solution.py:305
  373.1 9.2 %all_to_all.50 = bf16[8,32,128]{2,1,0:T(8,128)(2,1)} all-to-all(bf16[8,32,128]{2,1,0:T(8,128)(2,1)} %bitcast.20), channel_id=1, replica_groups=mesh['lat'=4,'lon'=8] {'lon'}, dimensions={0} | all-to-all | bytes 131072 | tf_op jit(solution)/shard_map/all_to_all | solution.py:470
  384.8 9.0 %all_to_all.51 = bf16[8,32,128]{2,1,0:T(8,128)(2,1)} all-to-all(bf16[8,32,128]{2,1,0:T(8,128)(2,1)} %bitcast.22), channel_id=1, replica_groups=mesh['lat'=4,'lon'=8] {'lon'}, dimensions={0} | all-to-all | bytes 131072 | tf_op jit(solution)/shard_map/all_to_all | solution.py:477
  (60 shorter events, 66.0 us)
Async XLA Ops:
  22.6 34.2 %all-to-all-start = ((bf16[4,1120,128]{2,1,0:T(8,128)(2,1)}), bf16[4,1120,128]{2,1,0:T(8,128)(2,1)S(1)}, u32[]{:S(2)}, u32[]{:S(2)}) async-start(bf16[4,1120,128]{2,1,0:T(8,128)(2,1)} %latitude.4), calls=%async_computation | async-start | bytes 2293760 | tf_op jit(solution)/shard_map/all_to_all | solution.py:450
  56.8 55.3 %copy-start.6 = (bf16[4,1120,128]{2,1,0:T(8,128)(2,1)}, bf16[4,1120,128]{2,1,0:T(8,128)(2,1)S(1)}, u32[]{:S(2)}) copy-start(bf16[4,1120,128]{2,1,0:T(8,128)(2,1)S(1)} %all-to-all-done.r_ref) | copy-start | bytes 3440644
  56.8 41.5 %all-to-all-start.2 = ((bf16[4,1600,128]{2,1,0:T(8,128)(2,1)}), bf16[4,1600,128]{2,1,0:T(8,128)(2,1)S(1)}, u32[]{:S(2)}, u32[]{:S(2)}) async-start(bf16[4,1600,128]{2,1,0:T(8,128)(2,1)} %latitude.5), calls=%async_computation.2 | async-start | bytes 3276800 | tf_op jit(solution)/shard_map/all_to_all | solution.py:450
  69.3 83.1 %copy-start.7 = (s32[640]{0:T(1024)S(1)}, s32[640]{0:T(1024)}, u32[]{:S(2)}) copy-start(s32[640]{0:T(1024)} %param.15) | copy-start | bytes 7684
  69.3 83.7 %copy-start.8 = (s32[2,768]{1,0:T(2,128)S(1)}, s32[2,768]{1,0:T(2,128)}, u32[]{:S(2)}) copy-start(s32[2,768]{1,0:T(2,128)} %constant.67.clone) | copy-start | bytes 18436
  98.3 1.2 copy-start.5
  99.5 48.5 %all-to-all-start.4 = ((bf16[4,1920,128]{2,1,0:T(8,128)(2,1)}), bf16[4,1920,128]{2,1,0:T(8,128)(2,1)S(1)}, u32[]{:S(2)}, u32[]{:S(2)}) async-start(bf16[4,1920,128]{2,1,0:T(8,128)(2,1)} %latitude.6), calls=%async_computation.4 | async-start | bytes 3932160 | tf_op jit(solution)/shard_map/all_to_all | solution.py:450
  148.0 51.3 %copy-start.4 = (bf16[4,1920,128]{2,1,0:T(8,128)(2,1)}, bf16[4,1920,128]{2,1,0:T(8,128)(2,1)S(1)}, u32[]{:S(2)}) copy-start(bf16[4,1920,128]{2,1,0:T(8,128)(2,1)S(1)} %all-to-all-done.4.r_ref) | copy-start | bytes 5898244
  148.0 51.3 %all-to-all-start.6 = ((bf16[4,1920,128]{2,1,0:T(8,128)(2,1)}), bf16[4,1920,128]{2,1,0:T(8,128)(2,1)}, u32[]{:S(2)}, u32[]{:S(2)}) async-start(bf16[4,1920,128]{2,1,0:T(8,128)(2,1)} %latitude.7), calls=%async_computation.6 | async-start | bytes 3932160 | tf_op jit(solution)/shard_map/all_to_all | solution.py:450
  199.3 28.9 %all-to-all-start.3 = ((bf16[8,960,128]{2,1,0:T(8,128)(2,1)}), bf16[8,960,128]{2,1,0:T(8,128)(2,1)S(1)}, u32[]{:S(2)}, u32[]{:S(2)}) async-start(bf16[8,960,128]{2,1,0:T(8,128)(2,1)} %longitude.5), calls=%async_computation.3 | async-start | bytes 3932160 | tf_op jit(solution)/shard_map/all_to_all | solution.py:457
  210.8 62.2 %copy-start.9 = (s32[1,1,12,1]{2,3,1,0:T(1,128)S(1)}, s32[1,1,12,1]{2,3,1,0:T(1,128)}, u32[]{:S(2)}) copy-start(s32[1,1,12,1]{2,3,1,0:T(1,128)} %param.19) | copy-start | bytes 148
  228.2 1.3 copy-start.1
  229.5 33.0 %all-to-all-start.5 = ((bf16[8,1152,128]{2,1,0:T(8,128)(2,1)}), bf16[8,1152,128]{2,1,0:T(8,128)(2,1)S(1)}, u32[]{:S(2)}, u32[]{:S(2)}) async-start(bf16[8,1152,128]{2,1,0:T(8,128)(2,1)} %longitude.6), calls=%async_computation.5 | async-start | bytes 4718592 | tf_op jit(solution)/shard_map/all_to_all | solution.py:457
  262.5 20.4 %copy-start = (bf16[8,1152,128]{2,1,0:T(8,128)(2,1)}, bf16[8,1152,128]{2,1,0:T(8,128)(2,1)S(1)}, u32[]{:S(2)}) copy-start(bf16[8,1152,128]{2,1,0:T(8,128)(2,1)S(1)} %all-to-all-done.5.refs_0_.refs_1_.refs_3_.refs_4_) | copy-start | bytes 7077892
  262.5 34.4 %all-to-all-start.7 = ((bf16[8,1152,128]{2,1,0:T(8,128)(2,1)}), bf16[8,1152,128]{2,1,0:T(8,128)(2,1)}, u32[]{:S(2)}, u32[]{:S(2)}) async-start(bf16[8,1152,128]{2,1,0:T(8,128)(2,1)} %longitude.7), calls=%async_computation.7 | async-start | bytes 4718592 | tf_op jit(solution)/shard_map/all_to_all | solution.py:457
  267.8 6.1 %collective-permute-start = (bf16[2,1,160,128]{3,2,1,0:T(8,128)(2,1)S(1)}, bf16[2,1,160,128]{3,2,1,0:T(8,128)(2,1)S(1)}, u32[]{:S(2)}, u32[]{:S(2)}) collective-permute-start(bf16[2,1,160,128]{3,2,1,0:T(8,128)(2,1)S(1)} %get-tuple-element.5), channel_id=1, source_target_pairs={{0,8},{8,16},{16,24},{1,9},{9,17},{17,25},{2,10},{10,18},{18,26},{... | collective-permute-start | bytes 245768 | tf_op jit(solution)/shard_map/ppermute | solution.py:401
  271.7 11.2 %collective-permute-start.1 = (bf16[2,1,160,128]{3,2,1,0:T(8,128)(2,1)S(1)}, bf16[2,1,160,128]{3,2,1,0:T(8,128)(2,1)S(1)}, u32[]{:S(2)}, u32[]{:S(2)}) collective-permute-start(bf16[2,1,160,128]{3,2,1,0:T(8,128)(2,1)S(1)} %get-tuple-element.4), channel_id=1, source_target_pairs={{8,0},{16,8},{24,16},{9,1},{17,9},{25,17},{10,2},{18,10},{26,18},{... | collective-permute-start | bytes 245768 | tf_op jit(solution)/shard_map/ppermute | solution.py:402
  282.9 4.9 %copy-start.2 = (bf16[2,162,160,128]{3,2,1,0:T(8,128)(2,1)}, bf16[2,162,160,128]{3,2,1,0:T(8,128)(2,1)S(1)}, u32[]{:S(2)}) copy-start(bf16[2,162,160,128]{3,2,1,0:T(8,128)(2,1)S(1)} %constant_dynamic-update-slice_fusion) | copy-start | bytes 39813124
  288.0 12.5 %collective-permute-start.3 = (bf16[2,162,1,128]{3,2,1,0:T(2,128)(2,1)S(1)}, bf16[2,162,1,128]{3,2,1,0:T(2,128)(2,1)S(1)}, u32[]{:S(2)}, u32[]{:S(2)}) collective-permute-start(bf16[2,162,1,128]{3,2,1,0:T(2,128)(2,1)S(1)} %get-tuple-element.3), channel_id=1, source_target_pairs={{1,0},{2,1},{3,2},{4,3},{5,4},{6,5},{7,6},{0,7},{9,8},{10,9},{11,1... | collective-permute-start | bytes 248840 | tf_op jit(solution)/shard_map/ppermute | solution.py:407
  289.6 10.8 %collective-permute-start.2 = (bf16[2,162,1,128]{3,2,1,0:T(2,128)(2,1)S(1)}, bf16[2,162,1,128]{3,2,1,0:T(2,128)(2,1)S(1)}, u32[]{:S(2)}, u32[]{:S(2)}) collective-permute-start(bf16[2,162,1,128]{3,2,1,0:T(2,128)(2,1)S(1)} %get-tuple-element.2), channel_id=1, source_target_pairs={{0,1},{1,2},{2,3},{3,4},{4,5},{5,6},{6,7},{7,0},{8,9},{9,10},{10,1... | collective-permute-start | bytes 248840 | tf_op jit(solution)/shard_map/ppermute | solution.py:406
  296.9 60.4 %all-to-all-start.1 = ((bf16[8,672,128]{2,1,0:T(8,128)(2,1)}), bf16[8,672,128]{2,1,0:T(8,128)(2,1)S(1)}, u32[]{:S(2)}, u32[]{:S(2)}) async-start(bf16[8,672,128]{2,1,0:T(8,128)(2,1)} %longitude.4), calls=%async_computation.1 | async-start | bytes 2752512 | tf_op jit(solution)/shard_map/all_to_all | solution.py:457
  357.3 1.1 copy-start.3
